TPU v7x, 32 devices: a whole 2x2x4 slice. The times are simulated.
32 devices in a mesh: dp: 8 (over z, y), col: 4 (over x, core).
Axes of the slice: x: 2, y: 2, z: 4, core: 2. Of those that a mesh axis runs over, the one named last changes fastest.
Arguments:
- tokens: bfloat16 [8192, 8192], P('dp', 'col'), may hold values from -6 to 6
- out_grad: bfloat16 [8192, 8192], P(('dp', 'col')), may hold values from -6 to 6
- weight: float32 [8192, 8192], P('dp', 'col'), may hold values from -6 to 6
- second: float32 [8192, 8192], P('dp', 'col'), may hold values from 0.0001 to 0.001
- momentum: float32 [8192, 512], P(('dp', 'col')), may hold values from -0.12 to 0.12
- sign_seed: int32 [1], replicated, may hold values from 0 to 999999
- step_number: int32 [1], replicated, may hold values from 1 to 999999
Outputs:
- new_weight: float32 [8192, 8192], P('dp', 'col')
- new_second: float32 [8192, 8192], P('dp', 'col')
- new_momentum: float32 [8192, 512], P(('dp', 'col'))
All inputs are finite; a program needn't handle non-finite values.
Results may differ from a plain program's by a relative error of at most 0.00097.
Values may be sent and summed in bfloat16 or wider, within the bound.
No kernel may reach another device: no remote copies, remote signals or barrier semaphores. Data moves between devices by JAX's collectives and lax.ppermute only.
A program may use at most 128 MiB of HBM per device.

v0:
```python
import jax
import jax.numpy as jnp
from jax import lax
from jax.sharding import PartitionSpec as P


def sign_table(sign_seed, step_number, first_row, row_count, low_rank):
    row_ids = first_row + lax.iota(jnp.int32, row_count)
    col_ids = lax.iota(jnp.int32, low_rank)
    flat_index = row_ids[:, None] * low_rank + col_ids[None, :]
    hashed = flat_index * 747796405 + sign_seed[0] * 1664525 + step_number[0] * 1013904223
    hashed = hashed ^ hashed >> 16 & 65535
    hashed = hashed * 2127912213
    hashed = hashed ^ hashed >> 13 & 524287
    hashed = hashed * 1103515245
    hashed = hashed ^ hashed >> 16 & 65535
    low_bit = hashed >> 20 & 1
    return (1 - 2 * low_bit).astype(jnp.float32)


def contract(left_rows, right_rows):
    return lax.dot_general(
        left_rows, right_rows, (((0,), (0,)), ((), ())), preferred_element_type=jnp.float32
    )


def per_device(tokens, out_grad, weight, second, momentum, sign_seed, step_number):
    local_tokens, din_local = tokens.shape
    low_rank = momentum.shape[1]
    owner_rows = momentum.shape[0]
    inv_root = 1.0 / jnp.sqrt(jnp.float32(low_rank))
    col_position = lax.axis_index("col")
    sign_block = sign_table(sign_seed, step_number, col_position * din_local, din_local, low_rank)
    partial_sketch = (
        jnp.dot(tokens, sign_block.astype(jnp.bfloat16), preferred_element_type=jnp.float32)
        * inv_root
    )
    quarter = lax.psum_scatter(partial_sketch, "col", scatter_dimension=0, tiled=True)
    sketch = quarter.astype(jnp.bfloat16)
    total_tokens = lax.axis_size("dp") * local_tokens
    data_count = lax.axis_size("dp")
    col_count = lax.axis_size("col")
    quarter_rows = out_grad.shape[0]
    grouped = out_grad.reshape(quarter_rows, data_count, col_count, owner_rows)
    grouped = jnp.transpose(grouped, (0, 2, 1, 3)).reshape(
        quarter_rows, col_count, data_count * owner_rows
    )
    regrouped = lax.all_to_all(grouped, "col", split_axis=1, concat_axis=0, tiled=True)
    regrouped = regrouped.reshape(quarter_rows * col_count, data_count * owner_rows)
    shard_sketch = lax.all_gather(sketch, "col", axis=0, tiled=True)
    projected = lax.psum_scatter(
        contract(regrouped, shard_sketch), "dp", scatter_dimension=0, tiled=True
    )
    projected = projected / jnp.float32(total_tokens)
    new_momentum = 0.8 * momentum + 0.2 * projected
    row_block = lax.all_gather(new_momentum, "col", axis=0, tiled=True)
    dense_grad = (
        lax.dot_general(
            row_block,
            sign_block,
            (((1,), (1,)), ((), ())),
            precision=lax.Precision.HIGHEST,
            preferred_element_type=jnp.float32,
        )
        * inv_root
    )
    new_second = 0.95 * second + 0.05 * dense_grad * dense_grad
    new_weight = weight - 0.5 * dense_grad / (jnp.sqrt(new_second) + 1e-08)
    return (new_weight, new_second, new_momentum)


def solution(mesh):
    placed = (
        P("dp", "col"),
        P(("dp", "col"), None),
        P("dp", "col"),
        P("dp", "col"),
        P(("dp", "col"), None),
        P(),
        P(),
    )
    return jax.shard_map(
        per_device,
        mesh=mesh,
        in_specs=placed,
        out_specs=(P("dp", "col"), P("dp", "col"), P(("dp", "col"), None)),
        check_vma=False,
    )
```

profile of v0, /device:TPU:0, one launch (start us, length us, event | category | flops | bytes accessed | tf_op | source)
XLA Modules:
  0.0 263.5 jit_solution(1373859997120523536)
XLA Ops:
  7.2 0.0 reduce-scatter.3.cloned.1.call-start
  8.5 7.7 %multiply_bitcast_fusion = f32[1024,512]{0,1:T(8,128)} fusion(bf16[1024,2048]{1,0:T(8,128)(2,1)} %param.7, s32[]{:T(128)} %bitcast.1, s32[]{:T(128)} %bitcast, s32[2048]{0:T(1024)S(1)} %add_multiply_fusion), kind=kOutput, calls=%fused_computation.9 | convolution fusion | flops 2170028032 | bytes 6299656 | tf_op jit(solution)/shard_map/dot_general | solution.py:35
  16.2 0.0 reduce-scatter.3.cloned.1.call-update
  16.3 7.8 %reshape.26 = bf16[256,8,4,256]{3,2,1,0:T(4,128)(2,1)} reshape(bf16[256,8192]{1,0:T(8,128)(2,1)} %param.8) | data formatting | bytes 8388608 | tf_op jit(solution)/shard_map/reshape | solution.py:44
  24.1 4.9 %copy.16 = bf16[256,8,4,256]{3,1,0,2:T(8,128)(2,1)} copy(bf16[256,8,4,256]{3,2,1,0:T(4,128)(2,1)} %reshape.26) | data formatting | bytes 8388608 | tf_op jit(solution)/shard_map/reshape | solution.py:44
  29.0 7.4 %reshape.27 = bf16[256,4,2048]{2,0,1:T(8,128)(2,1)} reshape(bf16[256,4,8,256]{3,2,0,1:T(8,128)(2,1)} %bitcast.22) | data formatting | bytes 8388608 | tf_op jit(solution)/shard_map/reshape | solution.py:45
  36.3 4.8 %all-to-all-start = ((bf16[256,4,2048]{2,0,1:T(8,128)(2,1)}), bf16[256,4,2048]{2,0,1:T(8,128)(2,1)}, u32[]{:S(2)}, u32[]{:S(2)}) async-start(bf16[256,4,2048]{2,0,1:T(8,128)(2,1)} %reshape.27), calls=%async_computation.1 | async-start | bytes 8388608 | tf_op jit(solution)/shard_map/all_to_all | solution.py:48
  41.2 0.0 all-gather.3.cloned.1.call-start
  41.2 12.6 %reduce-scatter.3.cloned.1.call-done = f32[256,512]{0,1:T(8,128)} async-done(((f32[1024,512]{0,1:T(8,128)}), f32[256,512]{0,1:T(8,128)}) %reduce-scatter.3.cloned.1.call-update) | async-done | bytes 524304 | tf_op jit(solution)/shard_map/reduce_scatter | solution.py:38
  53.8 1.8 convert_element_type.11
  55.6 0.0 all-gather.3.cloned.1.call-update
  55.6 0.0 reduce-scatter.5.cloned.1.call-start
  55.7 44.1 %all-to-all-done = bf16[256,4,2048]{2,0,1:T(8,128)(2,1)} async-done(((bf16[256,4,2048]{2,0,1:T(8,128)(2,1)}), bf16[256,4,2048]{2,0,1:T(8,128)(2,1)}, u32[]{:S(2)}, u32[]{:S(2)}) %all-to-all-start) | async-done | bytes 4194336 | tf_op jit(solution)/shard_map/all_to_all | solution.py:48
  99.7 0.0 all-gather.3.cloned.1.call-done
  99.7 6.9 %convolution_bitcast_fusion = f32[2048,512]{0,1:T(8,128)} fusion(bf16[1024,512]{0,1:T(8,128)(2,1)} %all-gather.3.cloned.1.call-done, bf16[1024,2048]{1,0:T(8,128)(2,1)} %bitcast.6), kind=kOutput, calls=%fused_computation.7 | convolution fusion | flops 2147483648 | bytes 9437184 | tf_op jit(solution)/shard_map/dot_general | solution.py:22
  106.6 0.0 copy-start
  106.6 0.0 reduce-scatter.5.cloned.1.call-update
  106.6 0.2 all-gather.5.cloned.1.call-start
  106.9 0.8 copy-done
  107.6 0.2 copy.12
  107.8 87.7 %reduce-scatter.5.cloned.1.call-done = f32[256,512]{0,1:T(8,128)} async-done(((f32[2048,512]{0,1:T(8,128)}), f32[256,512]{0,1:T(8,128)}) %reduce-scatter.5.cloned.1.call-update) | async-done | bytes 524304 | tf_op jit(solution)/shard_map/reduce_scatter | solution.py:51
  195.5 1.9 multiply_add_fusion.1
  197.5 0.0 all-gather.5.cloned.1.call-update
  197.5 2.0 copy.14
  199.5 20.3 %all-gather.5.cloned.1.call-done = f32[1024,512]{0,1:T(8,128)} async-done(((f32[256,512]{0,1:T(8,128)}), f32[1024,512]{0,1:T(8,128)}) %all-gather.5.cloned.1.call-update) | async-done | bytes 2097168 | tf_op jit(solution)/shard_map/all_gather | solution.py:56
  219.8 37.1 %divide_subtract_fusion = (f32[1024,2048]{1,0:T(8,128)}, f32[1024,2048]{1,0:T(8,128)}) fusion(f32[1024,2048]{1,0:T(8,128)} %param.9, f32[1024,2048]{1,0:T(8,128)} %param.10, f32[1024,512]{0,1:T(8,128)} %all-gather.5.cloned.1.call-done, s32[]{:T(128)} %bitcast.1, s32[]{:T(128)} %bitcast, s32[2048]{0:T(1024)S(1)} %add_multiply_fusion), kind=kOutput, calls=%fused_computation | convolution fusion | flops 12924747776 | bytes 35659784 | tf_op jit(solution)/shard_map/dot_general | solution.py:58
  (1 shorter events, 0.0 us)
Async XLA Ops:
  7.2 46.7 %reduce-scatter.3.cloned.1.call-start = ((), (), s32[]{:S(2)}) async-start(), calls=%async_computation.3 | async-start | bytes 2621440 | tf_op jit(solution)/shard_map/reduce_scatter | solution.py:38
  36.3 63.4 %all-to-all-start = ((bf16[256,4,2048]{2,0,1:T(8,128)(2,1)}), bf16[256,4,2048]{2,0,1:T(8,128)(2,1)}, u32[]{:S(2)}, u32[]{:S(2)}) async-start(bf16[256,4,2048]{2,0,1:T(8,128)(2,1)} %reshape.27), calls=%async_computation.1 | async-start | bytes 8388608 | tf_op jit(solution)/shard_map/all_to_all | solution.py:48
  41.2 58.5 %all-gather.3.cloned.1.call-start = ((), (), s32[]{:S(2)}) async-start(), calls=%async_computation.4 | async-start | bytes 1310720 | tf_op jit(solution)/shard_map/all_gather | solution.py:50
  55.6 139.9 %reduce-scatter.5.cloned.1.call-start = ((), (), s32[]{:S(2)}) async-start(), calls=%async_computation.5 | async-start | bytes 4718592 | tf_op jit(solution)/shard_map/reduce_scatter | solution.py:51
  106.6 1.0 copy-start
  106.6 113.2 %all-gather.5.cloned.1.call-start = ((), (), s32[]{:S(2)}) async-start(), calls=%async_computation.6 | async-start | bytes 2621440 | tf_op jit(solution)/shard_map/all_gather | solution.py:56
Sparse Core Ops, SparseCore 0:
  16.4 37.4 reduce-scatter.2
  56.0 21.9 all-gather.2
  106.7 88.7 reduce-scatter.4
  197.6 22.1 all-gather.4
where the time goes:
time: 264 us; the launch traced here: 263 us
  waiting for transfers between devices  165 us (62%)
  matrix products  51.7 us (20%)
  local copies, waits for them, and re-layouts  23.1 us (9%)
  between operations  15.1 us (6%)
  starting transfers between devices  5.19 us (2%)
  other arithmetic  3.69 us (1%)
    reduce_scatter x1, waiting for transfers between devices, per_device(): lax.psum_scatter(contract(regrouped, shard_sketch), 'dp', scatter_dimensi...  87.7 us
    all_to_all x1, waiting for transfers between devices, per_device(): lax.all_to_all(grouped, 'col', split_axis=1, concat_axis=0, tiled=True)  44.1 us
    dot_general x1, matrix products, per_device(): lax.dot_general(row_block, sign_block, (((1,), (1,)), ((), ())), precisio...  37.1 us
    all_gather x1, waiting for transfers between devices, per_device(): row_block = lax.all_gather(new_momentum, 'col', axis=0, tiled=True)  20.3 us
    reshape x2, local copies, waits for them, and re-layouts, per_device(): grouped = out_grad.reshape(quarter_rows, data_count, col_count, owner_rows)  12.7 us
    reduce_scatter x1, waiting for transfers between devices, per_device(): lax.psum_scatter(partial_sketch, 'col', scatter_dimension=0, tiled=True)  12.6 us
    dot_general x1, matrix products, per_device(): jnp.dot(tokens, sign_block.astype(jnp.bfloat16), preferred_element_type=j...  7.71 us
    reshape x1, local copies, waits for them, and re-layouts, per_device(): jnp.transpose(grouped, (0, 2, 1, 3))  7.37 us
  transfers between devices with their start and end apart: 5, of which 4 were waited for; matrix products, arithmetic and copies ran while one was open for 9% of the time, Pallas kernels for 0%

commit v1 on v0

--- a/solution.py
+++ b/solution.py
@@ -53,7 +53,13 @@
     )
     projected = projected / jnp.float32(total_tokens)
     new_momentum = 0.8 * momentum + 0.2 * projected
-    row_block = lax.all_gather(new_momentum, "col", axis=0, tiled=True)
+    size = lax.axis_size("col")
+    held, blocks = (new_momentum, [new_momentum])
+    for _ in range(size - 1):
+        held = lax.ppermute(held, "col", [(i, (i + 1) % size) for i in range(size)])
+        blocks.insert(0, held)
+    flat = jnp.concatenate(blocks, axis=0)
+    row_block = jnp.roll(flat, (lax.axis_index("col") + 1) * new_momentum.shape[0], axis=0)
     dense_grad = (
         lax.dot_general(
             row_block,

time: 264 us -> 267 us (1.011)
  waiting for transfers between devices: 165 us -> 169 us
    ppermute x0 -> x3, waiting for transfers between devices: none -> 24.8 us  [per_device(): held = lax.ppermute(held, 'col', [(i, (i + 1) % size) for i in range(size)])]
    all_gather x1 -> x0, waiting for transfers between devices: 20.3 us -> none  [per_device(): row_block = lax.all_gather(new_momentum, 'col', axis=0, tiled=True)]
  transfers between devices with their start and end apart: 5 -> 7, of which waited for: 4 -> 6; matrix products, arithmetic and copies ran while one was open for 9% -> 9% of each run, Pallas kernels for 0% -> 0%
where the time goes in v1:
time: 267 us; the launch traced here: 266 us
  waiting for transfers between devices  169 us (63%)
  matrix products  51 us (19%)
  local copies, waits for them, and re-layouts  22.8 us (9%)
  between operations  15.1 us (6%)
  starting transfers between devices  5.03 us (2%)
  other arithmetic  2.9 us (1%)
    reduce_scatter x1, waiting for transfers between devices, per_device(): lax.psum_scatter(contract(regrouped, shard_sketch), 'dp', scatter_dimensi...  87.7 us
    all_to_all x1, waiting for transfers between devices, per_device(): lax.all_to_all(grouped, 'col', split_axis=1, concat_axis=0, tiled=True)  44.1 us
    dot_general x1, matrix products, per_device(): lax.dot_general(row_block, sign_block, (((1,), (1,)), ((), ())), precisio...  36.5 us
    ppermute x3, waiting for transfers between devices, per_device(): held = lax.ppermute(held, 'col', [(i, (i + 1) % size) for i in range(size)])  24.8 us
    reshape x2, local copies, waits for them, and re-layouts, per_device(): grouped = out_grad.reshape(quarter_rows, data_count, col_count, owner_rows)  12.7 us
    reduce_scatter x1, waiting for transfers between devices, per_device(): lax.psum_scatter(partial_sketch, 'col', scatter_dimension=0, tiled=True)  12.6 us
    dot_general x1, matrix products, per_device(): jnp.dot(tokens, sign_block.astype(jnp.bfloat16), preferred_element_type=j...  7.71 us
    reshape x1, local copies, waits for them, and re-layouts, per_device(): jnp.transpose(grouped, (0, 2, 1, 3))  7.37 us
  transfers between devices with their start and end apart: 7, of which 6 were waited for; matrix products, arithmetic and copies ran while one was open for 9% of the time, Pallas kernels for 0%

profile of v1, /device:TPU:0, one launch (start us, length us, event | category | flops | bytes accessed | tf_op | source)
XLA Modules:
  0.0 266.1 jit_solution(16783042498085096468)
XLA Ops:
  7.2 0.0 reduce-scatter.3.cloned.1.call-start
  8.5 7.7 %multiply_bitcast_fusion = f32[1024,512]{0,1:T(8,128)} fusion(bf16[1024,2048]{1,0:T(8,128)(2,1)} %param.7, s32[]{:T(128)} %bitcast.1, s32[]{:T(128)} %bitcast, s32[2048]{0:T(1024)S(1)} %add_multiply_fusion), kind=kOutput, calls=%fused_computation.10 | convolution fusion | flops 2170028032 | bytes 6299656 | tf_op jit(solution)/shard_map/dot_general | solution.py:35
  16.2 0.0 reduce-scatter.3.cloned.1.call-update
  16.3 7.8 %reshape.26 = bf16[256,8,4,256]{3,2,1,0:T(4,128)(2,1)} reshape(bf16[256,8192]{1,0:T(8,128)(2,1)} %param.8) | data formatting | bytes 8388608 | tf_op jit(solution)/shard_map/reshape | solution.py:44
  24.1 4.9 %copy.16 = bf16[256,8,4,256]{3,1,0,2:T(8,128)(2,1)} copy(bf16[256,8,4,256]{3,2,1,0:T(4,128)(2,1)} %reshape.26) | data formatting | bytes 8388608 | tf_op jit(solution)/shard_map/reshape | solution.py:44
  29.0 7.4 %reshape.27 = bf16[256,4,2048]{2,0,1:T(8,128)(2,1)} reshape(bf16[256,4,8,256]{3,2,0,1:T(8,128)(2,1)} %bitcast.21) | data formatting | bytes 8388608 | tf_op jit(solution)/shard_map/reshape | solution.py:45
  36.3 4.8 %all-to-all-start = ((bf16[256,4,2048]{2,0,1:T(8,128)(2,1)}), bf16[256,4,2048]{2,0,1:T(8,128)(2,1)}, u32[]{:S(2)}, u32[]{:S(2)}) async-start(bf16[256,4,2048]{2,0,1:T(8,128)(2,1)} %reshape.27), calls=%async_computation.1 | async-start | bytes 8388608 | tf_op jit(solution)/shard_map/all_to_all | solution.py:48
  41.2 0.0 all-gather.2.cloned.1.call-start
  41.2 12.6 %reduce-scatter.3.cloned.1.call-done = f32[256,512]{0,1:T(8,128)} async-done(((f32[1024,512]{0,1:T(8,128)}), f32[256,512]{0,1:T(8,128)}) %reduce-scatter.3.cloned.1.call-update) | async-done | bytes 524304 | tf_op jit(solution)/shard_map/reduce_scatter | solution.py:38
  53.8 1.8 convert_element_type.11
  55.6 0.0 all-gather.2.cloned.1.call-update
  55.6 0.0 reduce-scatter.5.cloned.1.call-start
  55.7 44.1 %all-to-all-done = bf16[256,4,2048]{2,0,1:T(8,128)(2,1)} async-done(((bf16[256,4,2048]{2,0,1:T(8,128)(2,1)}), bf16[256,4,2048]{2,0,1:T(8,128)(2,1)}, u32[]{:S(2)}, u32[]{:S(2)}) %all-to-all-start) | async-done | bytes 4194336 | tf_op jit(solution)/shard_map/all_to_all | solution.py:48
  99.7 6.9 %convolution_bitcast_fusion = f32[2048,512]{0,1:T(8,128)} fusion(bf16[1024,512]{0,1:T(8,128)(2,1)} %all-gather.2.cloned.1.call-done, bf16[1024,2048]{1,0:T(8,128)(2,1)} %bitcast.6), kind=kOutput, calls=%fused_computation.7 | convolution fusion | flops 2147483648 | bytes 9437184 | tf_op jit(solution)/shard_map/dot_general | solution.py:22
  106.6 1.0 copy-done
  107.6 0.2 copy.12
  107.8 87.7 %reduce-scatter.5.cloned.1.call-done = f32[256,512]{0,1:T(8,128)} async-done(((f32[2048,512]{0,1:T(8,128)}), f32[256,512]{0,1:T(8,128)}) %reduce-scatter.5.cloned.1.call-update) | async-done | bytes 524304 | tf_op jit(solution)/shard_map/reduce_scatter | solution.py:51
  195.5 1.1 multiply_add_fusion.1
  196.7 0.1 collective-permute-start
  196.7 8.6 %collective-permute-done = f32[256,512]{0,1:T(8,128)S(1)} collective-permute-done((f32[256,512]{0,1:T(8,128)S(1)}, f32[256,512]{0,1:T(8,128)S(1)}, u32[]{:S(2)}, u32[]{:S(2)}) %collective-permute-start) | collective-permute-done | bytes 524320 | tf_op jit(solution)/shard_map/ppermute | solution.py:59
  205.3 8.6 %collective-permute-done.1 = f32[256,512]{0,1:T(8,128)S(1)} collective-permute-done((f32[256,512]{0,1:T(8,128)S(1)}, f32[256,512]{0,1:T(8,128)S(1)}, u32[]{:S(2)}, u32[]{:S(2)}) %collective-permute-start.1) | collective-permute-done | bytes 524320 | tf_op jit(solution)/shard_map/ppermute | solution.py:59
  213.9 1.0 copy.14
  214.9 7.6 %collective-permute-done.2 = f32[256,512]{0,1:T(8,128)S(1)} collective-permute-done((f32[256,512]{0,1:T(8,128)S(1)}, f32[256,512]{0,1:T(8,128)S(1)}, u32[]{:S(2)}, u32[]{:S(2)}) %collective-permute-start.2) | collective-permute-done | bytes 524320 | tf_op jit(solution)/shard_map/ppermute | solution.py:59
  222.5 0.1 constant_dynamic-update-slice_fusion.7
  222.6 0.1 constant_dynamic-update-slice_fusion.6
  222.7 0.1 constant_dynamic-update-slice_fusion.5
  222.8 0.1 constant_dynamic-update-slice_fusion.4
  222.8 0.1 constant_dynamic-update-slice_fusion.3
  222.9 0.1 constant_dynamic-update-slice_fusion.2
  223.0 0.1 constant_dynamic-update-slice_fusion.1
  223.1 0.1 constant_dynamic-update-slice_fusion
  223.2 36.5 %divide_subtract_fusion = (f32[1024,2048]{1,0:T(8,128)}, f32[1024,2048]{1,0:T(8,128)}) fusion(f32[1024,2048]{1,0:T(8,128)} %param.9, f32[1024,2048]{1,0:T(8,128)} %param.10, s32[]{:T(128)} %bitcast.1, s32[]{:T(128)} %bitcast, s32[2048]{0:T(1024)S(1)} %add_multiply_fusion, f32[2048,512]{0,1:T(8,128)S(1)} %constant_dynamic-update-slice_fusion, s32[]{:T(128)S(6)} %select_n.14), kind=kOutput, calls=%fused_computation | convolution fusion | flops 12924747776 | bytes 35659788 | tf_op jit(solution)/shard_map/dot_general | solution.py:64
  (6 shorter events, 0.0 us)
Async XLA Ops:
  7.2 46.7 %reduce-scatter.3.cloned.1.call-start = ((), (), s32[]{:S(2)}) async-start(), calls=%async_computation.3 | async-start | bytes 2621440 | tf_op jit(solution)/shard_map/reduce_scatter | solution.py:38
  36.3 63.4 %all-to-all-start = ((bf16[256,4,2048]{2,0,1:T(8,128)(2,1)}), bf16[256,4,2048]{2,0,1:T(8,128)(2,1)}, u32[]{:S(2)}, u32[]{:S(2)}) async-start(bf16[256,4,2048]{2,0,1:T(8,128)(2,1)} %reshape.27), calls=%async_computation.1 | async-start | bytes 8388608 | tf_op jit(solution)/shard_map/all_to_all | solution.py:48
  41.2 58.5 %all-gather.2.cloned.1.call-start = ((), (), s32[]{:S(2)}) async-start(), calls=%async_computation.4 | async-start | bytes 1310720 | tf_op jit(solution)/shard_map/all_gather | solution.py:50
  55.6 139.9 %reduce-scatter.5.cloned.1.call-start = ((), (), s32[]{:S(2)}) async-start(), calls=%async_computation.5 | async-start | bytes 4718592 | tf_op jit(solution)/shard_map/reduce_scatter | solution.py:51
  106.6 1.0 copy-start
  196.7 8.7 %collective-permute-start = (f32[256,512]{0,1:T(8,128)S(1)}, f32[256,512]{0,1:T(8,128)S(1)}, u32[]{:S(2)}, u32[]{:S(2)}) collective-permute-start(f32[256,512]{0,1:T(8,128)S(1)} %multiply_add_fusion.1), channel_id=1, source_target_pairs={{0,1},{1,2},{2,3},{3,0},{4,5},{5,6},{6,7},{7,4},{8,9},{9,10},{10,1... | collective-permute-start | bytes 1572872 | tf_op jit(solution)/shard_map/ppermute | solution.py:59
  205.3 8.6 %collective-permute-start.1 = (f32[256,512]{0,1:T(8,128)S(1)}, f32[256,512]{0,1:T(8,128)S(1)}, u32[]{:S(2)}, u32[]{:S(2)}) collective-permute-start(f32[256,512]{0,1:T(8,128)S(1)} %collective-permute-done), channel_id=1, source_target_pairs={{0,1},{1,2},{2,3},{3,0},{4,5},{5,6},{6,7},{7,4},{8,9},{9,10},{10,1... | collective-permute-start | bytes 1572872 | tf_op jit(solution)/shard_map/ppermute | solution.py:59
  213.9 8.6 %collective-permute-start.2 = (f32[256,512]{0,1:T(8,128)S(1)}, f32[256,512]{0,1:T(8,128)S(1)}, u32[]{:S(2)}, u32[]{:S(2)}) collective-permute-start(f32[256,512]{0,1:T(8,128)S(1)} %collective-permute-done.1), channel_id=1, source_target_pairs={{0,1},{1,2},{2,3},{3,0},{4,5},{5,6},{6,7},{7,4},{8,9},{9,10},{10,1... | collective-permute-start | bytes 1572872 | tf_op jit(solution)/shard_map/ppermute | solution.py:59
Sparse Core Ops, SparseCore 0:
  16.4 37.4 reduce-scatter.2
  56.0 21.9 all-gather.1
  106.7 88.7 reduce-scatter.4
